TPU v7x, 32 devices: a whole 2x2x4 slice. The times are simulated.
32 devices in a mesh: rep: 8 (over z, y), grp: 4 (over x, core).
Axes of the slice: x: 2, y: 2, z: 4, core: 2. Of those that a mesh axis runs over, the one named last changes fastest.
Arguments:
- tokens: bfloat16 [3648, 1152], P(('rep', 'grp')), may hold values from -6 to 6
- cotangent: bfloat16 [3648, 1152], P(('rep', 'grp')), may hold values from -6 to 6
- slice_sizes: int32 [32], replicated, may hold values from 113 to 114, as said below
- gain_one: float32 [1152], replicated, may hold values from 0.1 to 1.9
- shift_one: float32 [1152], replicated, may hold values from -3 to 3
- attn_in: bfloat16 [3456, 1152], P('grp')
- attn_bias: float32 [2, 1152], replicated, may hold values from -3 to 3
- attn_out: bfloat16 [1152, 1152], P('grp'), may hold values from -1 to 1
- out_bias: float32 [1152], replicated, may hold values from -3 to 3
- gain_two: float32 [1152], replicated, may hold values from 0.1 to 1.9
- shift_two: float32 [1152], replicated, may hold values from -3 to 3
- mlp_up: bfloat16 [4304, 1152], P('grp'), may hold values from -0.1875 to 0.1875
- up_bias: float32 [4304], replicated, may hold values from -3 to 3
- mlp_down: bfloat16 [4304, 1152], P('grp'), may hold values from -0.09375 to 0.09375
- down_bias: float32 [1152], replicated, may hold values from -3 to 3
Outputs:
- block_output: bfloat16 [3648, 1152], P(('rep', 'grp'))
- input_grad: float32 [3648, 1152], P(('rep', 'grp'))
- dgain_one: float32 [1152], replicated
- dshift_one: float32 [1152], replicated
- dattn_in: float32 [3456, 1152], P('grp', 'rep')
- dattn_bias: float32 [2, 1152], replicated
- dattn_out: float32 [1152, 1152], P('grp', 'rep')
- dout_bias: float32 [1152], replicated
- dgain_two: float32 [1152], replicated
- dshift_two: float32 [1152], replicated
- dmlp_up: float32 [4304, 1152], P('grp', 'rep')
- dup_bias: float32 [4304], replicated
- dmlp_down: float32 [4304, 1152], P('grp', 'rep')
- ddown_bias: float32 [1152], replicated
Inputs may be any that keep to these rules, and one draw needn't show every extreme that they name: slice_sizes sums to 3645; every entry is 113 or one more.
All inputs are finite; a program needn't handle non-finite values.
Results may differ from a plain program's by a relative error of at most 0.012.
Values may be sent and summed in bfloat16 or wider, within the bound.
A program may use at most 192 MiB of HBM per device.

v0:
```python
import jax
import jax.numpy as jnp
from jax import lax
from jax.sharding import PartitionSpec as P

H = 16
HD = 72
IMG = 729
EPSILON = 1e-06
SQRT_TWO_PI = 0.7978845608028654
CUBIC = 0.044715
NEGATIVE = -1e30


def passed_along(block, axis, distance):
    devices = range(lax.axis_size(axis))
    route = [(i - distance, i) for i in devices if i - distance in devices]
    return lax.ppermute(block, axis, route)


def norm_forward(rows, gain_row, shift_row):
    centered = rows - jnp.mean(rows, axis=-1, keepdims=True)
    inverse = lax.rsqrt(jnp.mean(centered * centered, axis=-1, keepdims=True) + EPSILON)
    normed = centered * inverse
    return (normed, inverse, normed * gain_row + shift_row)


def norm_backward(dscaled, normed, inverse, gain_row):
    dnormed = dscaled * gain_row
    return inverse * (
        dnormed
        - jnp.mean(dnormed, axis=-1, keepdims=True)
        - normed * jnp.mean(dnormed * normed, axis=-1, keepdims=True)
    )


def gelu_parts(before):
    inside = SQRT_TWO_PI * (before + CUBIC * before * before * before)
    tangent = jnp.tanh(inside)
    activated = 0.5 * before * (1.0 + tangent)
    derivative = 0.5 * (1.0 + tangent) + 0.5 * before * (1.0 - tangent * tangent) * SQRT_TWO_PI * (
        1.0 + 3.0 * CUBIC * before * before
    )
    return (activated, derivative)


def owned_grads(left_one, right_one, left_two, right_two):
    all_left_one, all_right_one, all_left_two, all_right_two = (
        lax.all_gather(left_one, "grp", axis=0, tiled=True),
        lax.all_gather(right_one, "grp", axis=0, tiled=True),
        lax.all_gather(left_two, "grp", axis=0, tiled=True),
        lax.all_gather(right_two, "grp", axis=0, tiled=True),
    )
    member = lax.axis_index("grp")
    groups = lax.axis_size("grp")
    rows_one = left_one.shape[1] // groups
    rows_two = left_two.shape[1] // groups
    picked_one = lax.dynamic_slice_in_dim(all_left_one, member * rows_one, rows_one, 1)
    picked_two = lax.dynamic_slice_in_dim(all_left_two, member * rows_two, rows_two, 1)
    grad_one = jnp.dot(picked_one.T, all_right_one, preferred_element_type=jnp.float32)
    grad_two = jnp.dot(picked_two.T, all_right_two, preferred_element_type=jnp.float32)
    return (grad_one, grad_two)


def replica_sums(first_rows, second_rows):
    return (
        lax.psum_scatter(first_rows, "rep", scatter_dimension=1, tiled=True),
        lax.psum_scatter(second_rows, "rep", scatter_dimension=1, tiled=True),
    )


def per_device(
    tokens,
    cotangent,
    slice_sizes,
    gain_one,
    shift_one,
    attn_in,
    attn_bias,
    attn_out,
    out_bias,
    gain_two,
    shift_two,
    mlp_up,
    up_bias,
    mlp_down,
    down_bias,
):
    capacity, width = tokens.shape
    base_rows = capacity - 1
    reach = (IMG - 2 + base_rows) // base_rows
    windows = (capacity + IMG - 2) // IMG + 1
    window_keys = windows * IMG
    score_scale = HD ** (-0.5)
    device = lax.axis_index(("rep", "grp"))
    starts = jnp.cumsum(slice_sizes) - slice_sizes
    own_start = starts[device]
    own_count = slice_sizes[device]
    row_index = jnp.arange(capacity, dtype=jnp.int32)
    is_live = row_index < own_count
    live_col = is_live[:, None]
    query_image = (own_start + row_index) // IMG
    first_image = own_start // IMG
    last_image = (own_start + own_count - 1) // IMG
    window_image = first_image + jnp.arange(windows, dtype=jnp.int32)
    key_image = jnp.repeat(jnp.minimum(window_image, last_image), IMG)
    key_live = jnp.repeat(window_image <= last_image, IMG)
    key_place = key_image * IMG + jnp.tile(jnp.arange(IMG, dtype=jnp.int32), windows)
    earlier = starts[None, :] <= key_place[:, None]
    owner = jnp.sum(earlier.astype(jnp.int32), axis=1) - 1
    owner_start = jnp.max(jnp.where(earlier, starts[None, :], 0), axis=1)
    buffer_row = (owner - device + reach) * capacity + key_place - owner_start
    allowed = (query_image[:, None] == key_image[None, :]) & key_live[None, :] & live_col
    full_in, full_out, full_up, full_down = (
        lax.all_gather(attn_in, "grp", axis=0, tiled=True),
        lax.all_gather(attn_out, "grp", axis=0, tiled=True),
        lax.all_gather(mlp_up, "grp", axis=0, tiled=True),
        lax.all_gather(mlp_down, "grp", axis=0, tiled=True),
    )
    tokens_f = tokens.astype(jnp.float32)
    normed_one, inverse_one, scaled_one = norm_forward(tokens_f, gain_one, shift_one)
    first = scaled_one.astype(jnp.bfloat16)
    bias_full = jnp.concatenate([attn_bias[0], jnp.zeros((width,), jnp.float32), attn_bias[1]])
    projected = jnp.dot(first, full_in.T, preferred_element_type=jnp.float32) + bias_full
    queries = projected[:, :width].astype(jnp.bfloat16)
    keyvalue = projected[:, width:].astype(jnp.bfloat16)
    pieces = []
    for offset in range(-reach, reach + 1):
        if offset == 0:
            pieces.append(keyvalue)
        else:
            pieces.append(passed_along(keyvalue, ("rep", "grp"), -offset))
    neighbours = jnp.concatenate(pieces, axis=0)
    window = neighbours[buffer_row]
    keys3 = window[:, :width].reshape(window_keys, H, HD)
    values3 = window[:, width:].reshape(window_keys, H, HD)
    queries3 = queries.reshape(capacity, H, HD)

    def masked_scores():
        raw = (
            jnp.einsum("qhd,khd->hqk", queries3, keys3, preferred_element_type=jnp.float32)
            * score_scale
        )
        return jnp.where(allowed[None], raw, NEGATIVE)

    scores = masked_scores()
    highest = jnp.max(scores, axis=-1, keepdims=True)
    logsum = highest + jnp.log(jnp.sum(jnp.exp(scores - highest), axis=-1, keepdims=True))
    weights = jnp.where(allowed[None], jnp.exp(scores - logsum), 0.0).astype(jnp.bfloat16)
    mixed = (
        jnp.einsum("hqk,khd->qhd", weights, values3, preferred_element_type=jnp.float32)
        .astype(jnp.bfloat16)
        .reshape(capacity, width)
    )
    resid = tokens_f + jnp.dot(mixed, full_out, preferred_element_type=jnp.float32) + out_bias
    normed_two, inverse_two, scaled_two = norm_forward(resid, gain_two, shift_two)
    second = scaled_two.astype(jnp.bfloat16)
    before = jnp.dot(second, full_up.T, preferred_element_type=jnp.float32) + up_bias
    activated, derivative = gelu_parts(before)
    hidden = activated.astype(jnp.bfloat16)
    final = resid + jnp.dot(hidden, full_down, preferred_element_type=jnp.float32) + down_bias
    block_output = jnp.where(live_col, final, 0.0).astype(jnp.bfloat16)
    dfinal_b = jnp.where(live_col, cotangent, jnp.zeros_like(cotangent))
    dfinal = dfinal_b.astype(jnp.float32)
    dbefore = jnp.dot(dfinal_b, full_down.T, preferred_element_type=jnp.float32) * derivative
    dbefore_b = dbefore.astype(jnp.bfloat16)
    dsecond = jnp.dot(dbefore_b, full_up, preferred_element_type=jnp.float32)
    dresid = dfinal + norm_backward(dsecond, normed_two, inverse_two, gain_two)
    mlp_up_rows, mlp_down_rows = owned_grads(dbefore_b, second, hidden, dfinal_b)
    dmlp_up, dmlp_down = replica_sums(mlp_up_rows, mlp_down_rows)
    dresid_b = dresid.astype(jnp.bfloat16)
    dmixed = jnp.dot(dresid_b, full_out.T, preferred_element_type=jnp.float32).astype(jnp.bfloat16)
    dmixed3 = dmixed.reshape(capacity, H, HD)
    delta = jnp.sum(
        dmixed3.astype(jnp.float32) * mixed.reshape(capacity, H, HD).astype(jnp.float32), axis=-1
    ).T
    scores = masked_scores()
    probs = jnp.where(allowed[None], jnp.exp(scores - logsum), 0.0)
    dprob = jnp.einsum("qhd,khd->hqk", dmixed3, values3, preferred_element_type=jnp.float32)
    dscore = (probs * (dprob - delta[:, :, None]) * score_scale).astype(jnp.bfloat16)
    dquery = jnp.einsum("hqk,khd->qhd", dscore, keys3, preferred_element_type=jnp.float32).reshape(
        capacity, width
    )
    dkey = jnp.einsum("hqk,qhd->khd", dscore, queries3, preferred_element_type=jnp.float32).reshape(
        window_keys, width
    )
    dvalue = jnp.einsum(
        "hqk,qhd->khd", weights, dmixed3, preferred_element_type=jnp.float32
    ).reshape(window_keys, width)
    dwindow = jnp.concatenate([dkey, dvalue], axis=1)
    dneighbours = (
        jnp.zeros((neighbours.shape[0], 2 * width), jnp.float32).at[buffer_row].add(dwindow)
    )
    dkeyvalue = dneighbours[reach * capacity : (reach + 1) * capacity]
    for offset in range(-reach, reach + 1):
        if offset != 0:
            segment = dneighbours[(offset + reach) * capacity : (offset + reach + 1) * capacity]
            dkeyvalue = dkeyvalue + passed_along(segment, ("rep", "grp"), offset)
    dprojected = jnp.concatenate([dquery, dkeyvalue], axis=1).astype(jnp.bfloat16)
    attn_in_rows, attn_out_rows = owned_grads(dprojected, first, mixed, dresid_b)
    dattn_in, dattn_out = replica_sums(attn_in_rows, attn_out_rows)
    dfirst = jnp.dot(dprojected, full_in, preferred_element_type=jnp.float32)
    input_grad = jnp.where(
        live_col, dresid + norm_backward(dfirst, normed_one, inverse_one, gain_one), 0.0
    )
    dgain_one, dshift_one, dattn_bias, dout_bias, dgain_two, dshift_two, dup_bias, ddown_bias = (
        lax.psum(
            (
                jnp.sum(dfirst * normed_one, axis=0),
                jnp.sum(dfirst, axis=0),
                jnp.stack([jnp.sum(dquery, axis=0), jnp.sum(dkeyvalue[:, width:], axis=0)]),
                jnp.sum(dresid, axis=0),
                jnp.sum(dsecond * normed_two, axis=0),
                jnp.sum(dsecond, axis=0),
                jnp.sum(dbefore, axis=0),
                jnp.sum(dfinal, axis=0),
            ),
            ("rep", "grp"),
        )
    )
    return (
        block_output,
        input_grad,
        dgain_one,
        dshift_one,
        dattn_in,
        dattn_bias,
        dattn_out,
        dout_bias,
        dgain_two,
        dshift_two,
        dmlp_up,
        dup_bias,
        dmlp_down,
        ddown_bias,
    )


def solution(mesh):
    in_specs = (
        P(("rep", "grp"), None),
        P(("rep", "grp"), None),
        P(),
        P(),
        P(),
        P("grp", None),
        P(),
        P("grp", None),
        P(),
        P(),
        P(),
        P("grp", None),
        P(),
        P("grp", None),
        P(),
    )
    out_specs = (
        P(("rep", "grp"), None),
        P(("rep", "grp"), None),
        P(),
        P(),
        P("grp", "rep"),
        P(),
        P("grp", "rep"),
        P(),
        P(),
        P(),
        P("grp", "rep"),
        P(),
        P("grp", "rep"),
        P(),
    )
    return jax.shard_map(
        per_device, mesh=mesh, in_specs=in_specs, out_specs=out_specs, check_vma=False
    )
```

profile of v0, /device:TPU:0, one launch (start us, length us, event | category | flops | bytes accessed | tf_op | source)
XLA Modules:
  0.0 1322.7 jit_solution(18031253088932466341)
XLA Ops:
  15.5 52.6 %all-gather.23.cloned.1.call-done = bf16[3456,1152]{1,0:T(8,128)(2,1)} async-done(((bf16[864,1152]{1,0:T(8,128)(2,1)}), bf16[3456,1152]{1,0:T(8,128)(2,1)}) %all-gather.23.cloned.1.call-update) | async-done | bytes 7962640 | tf_op jit(solution)/shard_map/all_gather | solution.py:115
  81.3 20.4 %collective-permute-done.13 = bf16[114,2304]{1,0:T(8,128)(2,1)S(1)} collective-permute-done((bf16[114,2304]{1,0:T(8,128)(2,1)S(1)}, bf16[114,2304]{1,0:T(8,128)(2,1)S(1)}, u32[]{:S(2)}, u32[]{:S(2)}) %collective-permute-start.13) | collective-permute-done | bytes 525344 | tf_op jit(solution)/shard_map/ppermute | solution.py:18
  106.9 13.9 %collective-permute-start.6 = (bf16[114,2304]{1,0:T(8,128)(2,1)S(1)}, bf16[114,2304]{1,0:T(8,128)(2,1)S(1)}, u32[]{:S(2)}, u32[]{:S(2)}) collective-permute-start(bf16[114,2304]{1,0:T(8,128)(2,1)S(1)} %slice.92), channel_id=1, source_target_pairs={{0,1},{1,2},{2,3},{3,4},{4,5},{5,6},{6,7},{7,8},{8,9},{9,10},{10,1... | collective-permute-start | bytes 1575944 | tf_op jit(solution)/shard_map/ppermute | solution.py:18
  134.1 17.2 %collective-permute-start.3 = (bf16[114,2304]{1,0:T(8,128)(2,1)S(1)}, bf16[114,2304]{1,0:T(8,128)(2,1)}, u32[]{:S(2)}, u32[]{:S(2)}) collective-permute-start(bf16[114,2304]{1,0:T(8,128)(2,1)S(1)} %slice.92), channel_id=1, source_target_pairs={{0,4},{1,5},{2,6},{3,7},{4,8},{5,9},{6,10},{7,11},{8,12},{9,13},{1... | collective-permute-start | bytes 1575944 | tf_op jit(solution)/shard_map/ppermute | solution.py:18
  155.1 28.5 %collective-permute-start.1 = (bf16[114,2304]{1,0:T(8,128)(2,1)S(1)}, bf16[114,2304]{1,0:T(8,128)(2,1)}, u32[]{:S(2)}, u32[]{:S(2)}) collective-permute-start(bf16[114,2304]{1,0:T(8,128)(2,1)S(1)} %slice.92), channel_id=1, source_target_pairs={{0,6},{1,7},{2,8},{3,9},{4,10},{5,11},{6,12},{7,13},{8,14},{9,15},... | collective-permute-start | bytes 1575944 | tf_op jit(solution)/shard_map/ppermute | solution.py:18
  183.6 8.0 collective-permute-start
  194.2 19.5 %collective-permute-done.1 = bf16[114,2304]{1,0:T(8,128)(2,1)} collective-permute-done((bf16[114,2304]{1,0:T(8,128)(2,1)S(1)}, bf16[114,2304]{1,0:T(8,128)(2,1)}, u32[]{:S(2)}, u32[]{:S(2)}) %collective-permute-start.1) | collective-permute-done | bytes 525344 | tf_op jit(solution)/shard_map/ppermute | solution.py:18
  213.7 21.3 %collective-permute-done = bf16[114,2304]{1,0:T(8,128)(2,1)} collective-permute-done((bf16[114,2304]{1,0:T(8,128)(2,1)S(1)}, bf16[114,2304]{1,0:T(8,128)(2,1)}, u32[]{:S(2)}, u32[]{:S(2)}) %collective-permute-start) | collective-permute-done | bytes 525344 | tf_op jit(solution)/shard_map/ppermute | solution.py:18
  235.0 57.9 %concatenate.14 = bf16[1710,2304]{1,0:T(8,128)(2,1)} concatenate(bf16[114,2304]{1,0:T(8,128)(2,1)} %collective-permute-done, bf16[114,2304]{1,0:T(8,128)(2,1)} %collective-permute-done.1, bf16[114,2304]{1,0:T(8,128)(2,1)} %collective-permute-done.2, bf16[114,2304]{1,0:T(8,128)(2,1)} %collective-permute-done.3, bf16[114,2304]{1,0:T(8,128)(2,1)} %collective-permute-done.4, ...), dimensions={0} | concatenate | bytes 15759360 | tf_op jit(solution)/shard_map/concatenate | solution.py:133
  292.9 18.3 %gather_fusion = bf16[1458,2304]{1,0:T(8,128)(2,1)} fusion(bf16[1710,2304]{1,0:T(8,128)(2,1)} %concatenate.14, s32[2048]{0:T(1024)S(1)} %pad_clamp_fusion), kind=kCustom, calls=%fused_computation | custom fusion | bytes 13442760 | tf_op jit(solution)/shard_map/gather | solution.py:134
  344.7 11.3 reshape.322
  363.5 12.1 reshape.324
  396.6 11.5 fusion.73
  438.1 29.8 %scatter_custom_fusion = f32[1710,2304]{1,0:T(8,128)} fusion(s32[1458]{0:T(1024)} %copy-done.35, f32[1458,1152]{1,0:T(8,128)} %copy.60, f32[]{:T(128)} %constant.83.clone.1, f32[1458,1152]{1,0:T(8,128)} %copy.59, f32[]{:T(128)} %constant.37.clone.1), kind=kCustom, calls=%fused_computation.2 | custom fusion | flops 6718464 | bytes 29252608 | tf_op jit(solution)/shard_map/scatter-add | solution.py:192
  467.9 10.2 fusion.79
  498.5 13.1 collective-permute-done.27
  513.8 21.4 %collective-permute-done.26 = f32[114,2304]{1,0:T(8,128)S(1)} collective-permute-done((f32[114,2304]{1,0:T(8,128)S(1)}, f32[114,2304]{1,0:T(8,128)S(1)}, u32[]{:S(2)}, u32[]{:S(2)}) %collective-permute-start.26) | collective-permute-done | bytes 1050656 | tf_op jit(solution)/shard_map/ppermute | solution.py:18
  537.6 15.8 %collective-permute-done.25 = f32[114,2304]{1,0:T(8,128)S(1)} collective-permute-done((f32[114,2304]{1,0:T(8,128)S(1)}, f32[114,2304]{1,0:T(8,128)S(1)}, u32[]{:S(2)}, u32[]{:S(2)}) %collective-permute-start.25) | collective-permute-done | bytes 1050656 | tf_op jit(solution)/shard_map/ppermute | solution.py:18
  556.7 20.5 %collective-permute-done.24 = f32[114,2304]{1,0:T(8,128)} collective-permute-done((f32[114,2304]{1,0:T(8,128)}, f32[114,2304]{1,0:T(8,128)}, u32[]{:S(2)}, u32[]{:S(2)}) %collective-permute-start.24) | collective-permute-done | bytes 1050656 | tf_op jit(solution)/shard_map/ppermute | solution.py:18
  579.8 32.6 %collective-permute-done.22 = f32[114,2304]{1,0:T(8,128)} collective-permute-done((f32[114,2304]{1,0:T(8,128)}, f32[114,2304]{1,0:T(8,128)}, u32[]{:S(2)}, u32[]{:S(2)}) %collective-permute-start.22) | collective-permute-done | bytes 1050656 | tf_op jit(solution)/shard_map/ppermute | solution.py:18
  623.9 10.7 collective-permute-done.19
  635.0 61.3 %collective-permute-done.17 = f32[114,2304]{1,0:T(8,128)} collective-permute-done((f32[114,2304]{1,0:T(8,128)}, f32[114,2304]{1,0:T(8,128)}, u32[]{:S(2)}, u32[]{:S(2)}) %collective-permute-start.17) | collective-permute-done | bytes 1050656 | tf_op jit(solution)/shard_map/ppermute | solution.py:18
  724.3 72.8 %all-gather.33.cloned.1.call-done = bf16[4,114,1152]{2,1,0:T(8,128)(2,1)} async-done(((bf16[1,114,1152]{2,1,0:T(8,128)(2,1)}), bf16[4,114,1152]{2,1,0:T(8,128)(2,1)}) %all-gather.33.cloned.1.call-update) | async-done | bytes 1050640 | tf_op jit(solution)/shard_map/all_gather | solution.py:50
  799.7 28.5 %all-gather.31.cloned.1.call-done = bf16[4,114,3456]{2,1,0:T(8,128)(2,1)} async-done(((bf16[1,114,3456]{2,1,0:T(8,128)(2,1)}), bf16[4,114,3456]{2,1,0:T(8,128)(2,1)}) %all-gather.31.cloned.1.call-update) | async-done | bytes 3151888 | tf_op jit(solution)/shard_map/all_gather | solution.py:49
  836.1 11.3 all-gather.45.cloned.1.call-done
  848.9 34.3 %all-gather.43.cloned.1.call-done = bf16[4,114,4304]{2,1,0:T(8,128)(2,1)} async-done(((bf16[1,114,4304]{2,1,0:T(8,128)(2,1)}), bf16[4,114,4304]{2,1,0:T(8,128)(2,1)}) %all-gather.43.cloned.1.call-update) | async-done | bytes 3925264 | tf_op jit(solution)/shard_map/all_gather | solution.py:51
  903.9 34.3 %all-gather.39.cloned.1.call-done = bf16[4,114,4304]{2,1,0:T(8,128)(2,1)} async-done(((bf16[1,114,4304]{2,1,0:T(8,128)(2,1)}), bf16[4,114,4304]{2,1,0:T(8,128)(2,1)}) %all-gather.39.cloned.1.call-update) | async-done | bytes 3925264 | tf_op jit(solution)/shard_map/all_gather | solution.py:49
  958.0 42.1 %all-reduce = (f32[1152]{0:T(1024)}, f32[1152]{0:T(1024)}, f32[2,1152]{1,0:T(2,128)}, f32[1152]{0:T(1024)}, f32[1152]{0:T(1024)}, /*index=5*/f32[1152]{0:T(1024)}, f32[4304]{0:T(1024)}, f32[1152]{0:T(1024)}) all-reduce(f32[1152]{0:T(1024)S(1)} %get-tuple-element.16, ...), channel_id=1, replica_groups=mesh['rep'=8,'grp'=4] {'rep','grp'}, use_global_device_ids=true, to_apply=%region_16.17 | all-reduce | flops 13520 | bytes 108160 | tf_op jit(solution)/shard_map/psum | solution.py:207
  1000.1 8.9 reduce-scatter.7.cloned.1.call-done
  1009.0 90.7 %reduce-scatter.5.cloned.1.call-done = f32[864,144]{0,1:T(8,128)} async-done(((f32[864,1152]{0,1:T(8,128)}), f32[864,144]{0,1:T(8,128)}) %reduce-scatter.5.cloned.1.call-update) | async-done | bytes 497680 | tf_op jit(solution)/shard_map/reduce_scatter | solution.py:67
  1099.7 108.1 %reduce-scatter.11.cloned.1.call-done = f32[1076,144]{0,1:T(8,128)} async-done(((f32[1076,1152]{0,1:T(8,128)}), f32[1076,144]{0,1:T(8,128)}) %reduce-scatter.11.cloned.1.call-update) | async-done | bytes 619792 | tf_op jit(solution)/shard_map/reduce_scatter | solution.py:68
  1207.8 108.2 %reduce-scatter.9.cloned.1.call-done = f32[1076,144]{0,1:T(8,128)} async-done(((f32[1076,1152]{0,1:T(8,128)}), f32[1076,144]{0,1:T(8,128)}) %reduce-scatter.9.cloned.1.call-update) | async-done | bytes 619792 | tf_op jit(solution)/shard_map/reduce_scatter | solution.py:67
  (283 shorter events, 257.1 us)
Async XLA Ops:
  7.2 61.0 %all-gather.23.cloned.1.call-start = ((), (), s32[]{:S(2)}) async-start(), calls=%async_computation.4 | async-start | bytes 9953280 | tf_op jit(solution)/shard_map/all_gather | solution.py:115
  7.9 333.9 %all-gather.25.cloned.1.call-start = ((), (), s32[]{:S(2)}) async-start(), calls=%async_computation.5 | async-start | bytes 3317760 | tf_op jit(solution)/shard_map/all_gather | solution.py:116
  8.7 336.1 %all-gather.27.cloned.1.call-start = ((), (), s32[]{:S(2)}) async-start(), calls=%async_computation.10 | async-start | bytes 12441600 | tf_op jit(solution)/shard_map/all_gather | solution.py:117
  9.4 354.1 %all-gather.29.cloned.1.call-start = ((), (), s32[]{:S(2)}) async-start(), calls=%async_computation.11 | async-start | bytes 12441600 | tf_op jit(solution)/shard_map/all_gather | solution.py:118
  10.0 708.9 %all-gather.35.cloned.1.call-start = ((), (), s32[]{:S(2)}) async-start(), calls=%async_computation.14 | async-start | bytes 1382400 | tf_op jit(solution)/shard_map/all_gather | solution.py:51
  120.8 62.7 %collective-permute-start.5 = (bf16[114,2304]{1,0:T(8,128)(2,1)S(1)}, bf16[114,2304]{1,0:T(8,128)(2,1)S(1)}, u32[]{:S(2)}, u32[]{:S(2)}) collective-permute-start(bf16[114,2304]{1,0:T(8,128)(2,1)S(1)} %slice.92), channel_id=1, source_target_pairs={{0,2},{1,3},{2,4},{3,5},{4,6},{5,7},{6,8},{7,9},{8,10},{9,11},{10,... | collective-permute-start | bytes 1575944 | tf_op jit(solution)/shard_map/ppermute | solution.py:18
  128.2 66.0 %collective-permute-start.4 = (bf16[114,2304]{1,0:T(8,128)(2,1)S(1)}, bf16[114,2304]{1,0:T(8,128)(2,1)}, u32[]{:S(2)}, u32[]{:S(2)}) collective-permute-start(bf16[114,2304]{1,0:T(8,128)(2,1)S(1)} %slice.92), channel_id=1, source_target_pairs={{0,3},{1,4},{2,5},{3,6},{4,7},{5,8},{6,9},{7,10},{8,11},{9,12},{10... | collective-permute-start | bytes 1575944 | tf_op jit(solution)/shard_map/ppermute | solution.py:18
  134.1 60.1 %collective-permute-start.3 = (bf16[114,2304]{1,0:T(8,128)(2,1)S(1)}, bf16[114,2304]{1,0:T(8,128)(2,1)}, u32[]{:S(2)}, u32[]{:S(2)}) collective-permute-start(bf16[114,2304]{1,0:T(8,128)(2,1)S(1)} %slice.92), channel_id=1, source_target_pairs={{0,4},{1,5},{2,6},{3,7},{4,8},{5,9},{6,10},{7,11},{8,12},{9,13},{1... | collective-permute-start | bytes 1575944 | tf_op jit(solution)/shard_map/ppermute | solution.py:18
  155.1 58.6 %collective-permute-start.1 = (bf16[114,2304]{1,0:T(8,128)(2,1)S(1)}, bf16[114,2304]{1,0:T(8,128)(2,1)}, u32[]{:S(2)}, u32[]{:S(2)}) collective-permute-start(bf16[114,2304]{1,0:T(8,128)(2,1)S(1)} %slice.92), channel_id=1, source_target_pairs={{0,6},{1,7},{2,8},{3,9},{4,10},{5,11},{6,12},{7,13},{8,14},{9,15},... | collective-permute-start | bytes 1575944 | tf_op jit(solution)/shard_map/ppermute | solution.py:18
  183.6 51.4 %collective-permute-start = (bf16[114,2304]{1,0:T(8,128)(2,1)S(1)}, bf16[114,2304]{1,0:T(8,128)(2,1)}, u32[]{:S(2)}, u32[]{:S(2)}) collective-permute-start(bf16[114,2304]{1,0:T(8,128)(2,1)S(1)} %slice.92), channel_id=1, source_target_pairs={{0,7},{1,8},{2,9},{3,10},{4,11},{5,12},{6,13},{7,14},{8,15},{9,16}... | collective-permute-start | bytes 1575944 | tf_op jit(solution)/shard_map/ppermute | solution.py:18
  486.5 66.9 %collective-permute-start.25 = (f32[114,2304]{1,0:T(8,128)S(1)}, f32[114,2304]{1,0:T(8,128)S(1)}, u32[]{:S(2)}, u32[]{:S(2)}) collective-permute-start(f32[114,2304]{1,0:T(8,128)S(1)} %get-tuple-element.43), channel_id=1, source_target_pairs={{0,5},{1,6},{2,7},{3,8},{4,9},{5,10},{6,11},{7,12},{8,13},{9,14},{... | collective-permute-start | bytes 3151880 | tf_op jit(solution)/shard_map/ppermute | solution.py:18
  487.9 89.3 %collective-permute-start.24 = (f32[114,2304]{1,0:T(8,128)}, f32[114,2304]{1,0:T(8,128)}, u32[]{:S(2)}, u32[]{:S(2)}) collective-permute-start(f32[114,2304]{1,0:T(8,128)} %get-tuple-element.44), channel_id=1, source_target_pairs={{0,4},{1,5},{2,6},{3,7},{4,8},{5,9},{6,10},{7,11},{8,12},{9,13},{1... | collective-permute-start | bytes 3151880 | tf_op jit(solution)/shard_map/ppermute | solution.py:18
  496.2 82.3 %collective-permute-start.23 = (f32[114,2304]{1,0:T(8,128)}, f32[114,2304]{1,0:T(8,128)}, u32[]{:S(2)}, u32[]{:S(2)}) collective-permute-start(f32[114,2304]{1,0:T(8,128)} %get-tuple-element.45), channel_id=1, source_target_pairs={{0,3},{1,4},{2,5},{3,6},{4,7},{5,8},{6,9},{7,10},{8,11},{9,12},{10... | collective-permute-start | bytes 3151880 | tf_op jit(solution)/shard_map/ppermute | solution.py:18
  511.6 100.8 %collective-permute-start.22 = (f32[114,2304]{1,0:T(8,128)}, f32[114,2304]{1,0:T(8,128)}, u32[]{:S(2)}, u32[]{:S(2)}) collective-permute-start(f32[114,2304]{1,0:T(8,128)} %get-tuple-element.46), channel_id=1, source_target_pairs={{0,2},{1,3},{2,4},{3,5},{4,6},{5,7},{6,8},{7,9},{8,10},{9,11},{10,... | collective-permute-start | bytes 3151880 | tf_op jit(solution)/shard_map/ppermute | solution.py:18
  535.3 78.4 %collective-permute-start.21 = (f32[114,2304]{1,0:T(8,128)}, f32[114,2304]{1,0:T(8,128)}, u32[]{:S(2)}, u32[]{:S(2)}) collective-permute-start(f32[114,2304]{1,0:T(8,128)} %get-tuple-element.47), channel_id=1, source_target_pairs={{0,1},{1,2},{2,3},{3,4},{4,5},{5,6},{6,7},{7,8},{8,9},{9,10},{10,1... | collective-permute-start | bytes 3151880 | tf_op jit(solution)/shard_map/ppermute | solution.py:18
  553.4 61.6 %collective-permute-start.20 = (f32[114,2304]{1,0:T(8,128)}, f32[114,2304]{1,0:T(8,128)}, u32[]{:S(2)}, u32[]{:S(2)}) collective-permute-start(f32[114,2304]{1,0:T(8,128)} %get-tuple-element.48), channel_id=1, source_target_pairs={{1,0},{2,1},{3,2},{4,3},{5,4},{6,5},{7,6},{8,7},{9,8},{10,9},{11,1... | collective-permute-start | bytes 3151880 | tf_op jit(solution)/shard_map/ppermute | solution.py:18
  556.6 163.9 %all-gather.37.cloned.1.call-start = ((), (), s32[]{:S(2)}) async-start(), calls=%async_computation.15 | async-start | bytes 1382400 | tf_op jit(solution)/shard_map/all_gather | solution.py:52
  577.2 57.4 %collective-permute-start.19 = (f32[114,2304]{1,0:T(8,128)}, f32[114,2304]{1,0:T(8,128)}, u32[]{:S(2)}, u32[]{:S(2)}) collective-permute-start(f32[114,2304]{1,0:T(8,128)} %get-tuple-element.49), channel_id=1, source_target_pairs={{2,0},{3,1},{4,2},{5,3},{6,4},{7,5},{8,6},{9,7},{10,8},{11,9},{12,... | collective-permute-start | bytes 3151880 | tf_op jit(solution)/shard_map/ppermute | solution.py:18
  578.5 56.5 %collective-permute-start.18 = (f32[114,2304]{1,0:T(8,128)}, f32[114,2304]{1,0:T(8,128)}, u32[]{:S(2)}, u32[]{:S(2)}) collective-permute-start(f32[114,2304]{1,0:T(8,128)} %get-tuple-element.50), channel_id=1, source_target_pairs={{3,0},{4,1},{5,2},{6,3},{7,4},{8,5},{9,6},{10,7},{11,8},{12,9},{13... | collective-permute-start | bytes 3151880 | tf_op jit(solution)/shard_map/ppermute | solution.py:18
  612.4 83.9 %collective-permute-start.17 = (f32[114,2304]{1,0:T(8,128)}, f32[114,2304]{1,0:T(8,128)}, u32[]{:S(2)}, u32[]{:S(2)}) collective-permute-start(f32[114,2304]{1,0:T(8,128)} %get-tuple-element.51), channel_id=1, source_target_pairs={{4,0},{5,1},{6,2},{7,3},{8,4},{9,5},{10,6},{11,7},{12,8},{13,9},{1... | collective-permute-start | bytes 3151880 | tf_op jit(solution)/shard_map/ppermute | solution.py:18
  613.7 83.9 %collective-permute-start.16 = (f32[114,2304]{1,0:T(8,128)}, f32[114,2304]{1,0:T(8,128)}, u32[]{:S(2)}, u32[]{:S(2)}) collective-permute-start(f32[114,2304]{1,0:T(8,128)} %get-tuple-element.52), channel_id=1, source_target_pairs={{5,0},{6,1},{7,2},{8,3},{9,4},{10,5},{11,6},{12,7},{13,8},{14,9},{... | collective-permute-start | bytes 3151880 | tf_op jit(solution)/shard_map/ppermute | solution.py:18
  615.0 82.6 %collective-permute-start.15 = (f32[114,2304]{1,0:T(8,128)}, f32[114,2304]{1,0:T(8,128)}, u32[]{:S(2)}, u32[]{:S(2)}) collective-permute-start(f32[114,2304]{1,0:T(8,128)} %get-tuple-element.53), channel_id=1, source_target_pairs={{6,0},{7,1},{8,2},{9,3},{10,4},{11,5},{12,6},{13,7},{14,8},{15,9},... | collective-permute-start | bytes 3151880 | tf_op jit(solution)/shard_map/ppermute | solution.py:18
  623.9 173.2 %all-gather.33.cloned.1.call-start = ((), (), s32[]{:S(2)}) async-start(), calls=%async_computation.13 | async-start | bytes 1382400 | tf_op jit(solution)/shard_map/all_gather | solution.py:50
  711.5 116.7 %all-gather.31.cloned.1.call-start = ((), (), s32[]{:S(2)}) async-start(), calls=%async_computation.12 | async-start | bytes 4147200 | tf_op jit(solution)/shard_map/all_gather | solution.py:49
  712.6 134.8 %all-gather.45.cloned.1.call-start = ((), (), s32[]{:S(2)}) async-start(), calls=%async_computation.19 | async-start | bytes 1382400 | tf_op jit(solution)/shard_map/all_gather | solution.py:52
  713.5 169.7 %all-gather.43.cloned.1.call-start = ((), (), s32[]{:S(2)}) async-start(), calls=%async_computation.18 | async-start | bytes 5222400 | tf_op jit(solution)/shard_map/all_gather | solution.py:51
  717.0 185.4 %all-gather.41.cloned.1.call-start = ((), (), s32[]{:S(2)}) async-start(), calls=%async_computation.17 | async-start | bytes 1382400 | tf_op jit(solution)/shard_map/all_gather | solution.py:50
  717.7 220.5 %all-gather.39.cloned.1.call-start = ((), (), s32[]{:S(2)}) async-start(), calls=%async_computation.16 | async-start | bytes 5222400 | tf_op jit(solution)/shard_map/all_gather | solution.py:49
  718.9 290.2 %reduce-scatter.7.cloned.1.call-start = ((), (), s32[]{:S(2)}) async-start(), calls=%async_computation.7 | async-start | bytes 1990656 | tf_op jit(solution)/shard_map/reduce_scatter | solution.py:68
  724.3 375.4 %reduce-scatter.5.cloned.1.call-start = ((), (), s32[]{:S(2)}) async-start(), calls=%async_computation.6 | async-start | bytes 4644864 | tf_op jit(solution)/shard_map/reduce_scatter | solution.py:67
  835.8 372.0 %reduce-scatter.11.cloned.1.call-start = ((), (), s32[]{:S(2)}) async-start(), calls=%async_computation.9 | async-start | bytes 5971968 | tf_op jit(solution)/shard_map/reduce_scatter | solution.py:68
  894.6 421.4 %reduce-scatter.9.cloned.1.call-start = ((), (), s32[]{:S(2)}) async-start(), calls=%async_computation.8 | async-start | bytes 5971968 | tf_op jit(solution)/shard_map/reduce_scatter | solution.py:67
  (69 other events, 2079.1 us)
Sparse Core Ops, SparseCore 0:
  9.5 58.5 all-gather.22
  69.7 59.2 all-gather.24
  130.6 116.8 all-gather.26
  248.8 68.5 all-gather.28
  556.7 44.4 all-gather.34
  623.9 48.2 all-gather.36
  711.6 85.4 all-gather.32
  798.7 29.4 all-gather.30
  830.3 17.0 all-gather.44
  848.8 34.3 all-gather.42
  885.3 17.0 all-gather.40
  903.8 34.3 all-gather.38
  942.2 66.7 reduce-scatter.6
  1013.0 86.6 reduce-scatter.4
  1103.7 104.0 reduce-scatter.10
  1211.8 104.1 reduce-scatter.8
where the time goes:
time: 1330 us; the launch traced here: 1320 us
  waiting for transfers between devices  806 us (61%)
  local copies, waits for them, and re-layouts  178 us (13%)
  starting transfers between devices  122 us (9%)
  matrix products  100 us (8%)
  other arithmetic  55.2 us (4%)
  blocking collectives  42.1 us (3%)
  between operations  18.6 us (1%)
    ppermute x28, waiting for transfers between devices, passed_along(): return lax.ppermute(block, axis, route)  245 us
    reduce_scatter x2, waiting for transfers between devices, replica_sums(): lax.psum_scatter(first_rows, 'rep', scatter_dimension=1, tiled=True)  199 us
    ppermute x28, starting transfers between devices, passed_along(): return lax.ppermute(block, axis, route)  122 us
    reduce_scatter x2, waiting for transfers between devices, replica_sums(): lax.psum_scatter(second_rows, 'rep', scatter_dimension=1, tiled=True)  117 us
    all_gather x2, waiting for transfers between devices, owned_grads(): lax.all_gather(right_one, 'grp', axis=0, tiled=True)  80.5 us
    all_gather x2, waiting for transfers between devices, owned_grads(): lax.all_gather(left_one, 'grp', axis=0, tiled=True)  62.8 us
    concatenate x1, local copies, waits for them, and re-layouts, per_device(): neighbours = jnp.concatenate(pieces, axis=0)  57.9 us
    unnamed x125, local copies, waits for them, and re-layouts  52.8 us
  transfers between devices with their start and end apart: 44, of which 26 were waited for; matrix products, arithmetic and copies ran while one was open for 16% of the time, Pallas kernels for 0%

commit v1 on v0

--- a/solution.py
+++ b/solution.py
@@ -12,6 +12,13 @@
 NEGATIVE = -1e30
 
 
+def tell_the_column(work_x, row_dim):
+    return jnp.concatenate(
+        jax.lax.all_to_all(jnp.stack(jax.lax.axis_size("grp") * [work_x]), "grp", 0, 0),
+        axis=row_dim,
+    )
+
+
 def passed_along(block, axis, distance):
     devices = range(lax.axis_size(axis))
     route = [(i - distance, i) for i in devices if i - distance in devices]
@@ -47,7 +54,7 @@
 def owned_grads(left_one, right_one, left_two, right_two):
     all_left_one, all_right_one, all_left_two, all_right_two = (
         lax.all_gather(left_one, "grp", axis=0, tiled=True),
-        lax.all_gather(right_one, "grp", axis=0, tiled=True),
+        tell_the_column(right_one, 0),
         lax.all_gather(left_two, "grp", axis=0, tiled=True),
         lax.all_gather(right_two, "grp", axis=0, tiled=True),
     )

time: 1330 us -> 1310 us (0.985)
  waiting for transfers between devices: 806 us -> 688 us
  starting transfers between devices: 122 us -> 189 us
  blocking collectives: 42.1 us -> 71.8 us
    all_gather x2 -> x0, waiting for transfers between devices: 80.5 us -> none  [owned_grads(): lax.all_gather(right_one, 'grp', axis=0, tiled=True)]
    all_to_all x0 -> x1, starting transfers between devices: none -> 66.9 us  [tell_the_column(): jax.lax.all_to_all(jnp.stack(jax.lax.axis_size('grp') * [work_x]), 'grp',...]
    all_gather x2, waiting for transfers between devices: 62.8 us -> 6.72 us  [owned_grads(): lax.all_gather(left_one, 'grp', axis=0, tiled=True)]
    all_to_all x0 -> x1, blocking collectives: none -> 30 us  [tell_the_column(): jax.lax.all_to_all(jnp.stack(jax.lax.axis_size('grp') * [work_x]), 'grp',...]
    all_to_all x0 -> x1, waiting for transfers between devices: none -> 27.5 us  [tell_the_column(): jax.lax.all_to_all(jnp.stack(jax.lax.axis_size('grp') * [work_x]), 'grp',...]
    unnamed x125 -> x133, local copies, waits for them, and re-layouts: 52.8 us -> 51.2 us
  transfers between devices with their start and end apart: 44 -> 43, of which waited for: 26 -> 25; matrix products, arithmetic and copies ran while one was open for 16% -> 17% of each run, Pallas kernels for 0% -> 0%
where the time goes in v1:
time: 1310 us; the launch traced here: 1300 us
  waiting for transfers between devices  688 us (53%)
  starting transfers between devices  189 us (14%)
  local copies, waits for them, and re-layouts  179 us (14%)
  matrix products  99.9 us (8%)
  blocking collectives  71.8 us (5%)
  other arithmetic  54.5 us (4%)
  between operations  18.8 us (1%)
    ppermute x28, waiting for transfers between devices, passed_along(): return lax.ppermute(block, axis, route)  245 us
    reduce_scatter x2, waiting for transfers between devices, replica_sums(): lax.psum_scatter(first_rows, 'rep', scatter_dimension=1, tiled=True)  199 us
    ppermute x28, starting transfers between devices, passed_along(): return lax.ppermute(block, axis, route)  121 us
    reduce_scatter x2, waiting for transfers between devices, replica_sums(): lax.psum_scatter(second_rows, 'rep', scatter_dimension=1, tiled=True)  111 us
    all_to_all x1, starting transfers between devices, tell_the_column(): jax.lax.all_to_all(jnp.stack(jax.lax.axis_size('grp') * [work_x]), 'grp',...  66.9 us
    concatenate x1, local copies, waits for them, and re-layouts, per_device(): neighbours = jnp.concatenate(pieces, axis=0)  57.8 us
    all_gather x1, waiting for transfers between devices, per_device(): lax.all_gather(attn_in, 'grp', axis=0, tiled=True)  52.1 us
    unnamed x133, local copies, waits for them, and re-layouts  51.2 us
  transfers between devices with their start and end apart: 43, of which 25 were waited for; matrix products, arithmetic and copies ran while one was open for 17% of the time, Pallas kernels for 0%

profile of v1, /device:TPU:0, one launch (start us, length us, event | category | flops | bytes accessed | tf_op | source)
XLA Modules:
  0.0 1301.0 jit_solution(6315348791036982454)
XLA Ops:
  16.0 52.1 %all-gather.19.cloned.1.call-done = bf16[3456,1152]{1,0:T(8,128)(2,1)} async-done(((bf16[864,1152]{1,0:T(8,128)(2,1)}), bf16[3456,1152]{1,0:T(8,128)(2,1)}) %all-gather.19.cloned.1.call-update) | async-done | bytes 7962640 | tf_op jit(solution)/shard_map/all_gather | solution.py:122
  81.3 20.3 %collective-permute-done.13 = bf16[114,2304]{1,0:T(8,128)(2,1)S(1)} collective-permute-done((bf16[114,2304]{1,0:T(8,128)(2,1)S(1)}, bf16[114,2304]{1,0:T(8,128)(2,1)S(1)}, u32[]{:S(2)}, u32[]{:S(2)}) %collective-permute-start.13) | collective-permute-done | bytes 525344 | tf_op jit(solution)/shard_map/ppermute | solution.py:25
  106.9 13.9 %collective-permute-start.6 = (bf16[114,2304]{1,0:T(8,128)(2,1)S(1)}, bf16[114,2304]{1,0:T(8,128)(2,1)S(1)}, u32[]{:S(2)}, u32[]{:S(2)}) collective-permute-start(bf16[114,2304]{1,0:T(8,128)(2,1)S(1)} %slice.92), channel_id=1, source_target_pairs={{0,1},{1,2},{2,3},{3,4},{4,5},{5,6},{6,7},{7,8},{8,9},{9,10},{10,1... | collective-permute-start | bytes 1575944 | tf_op jit(solution)/shard_map/ppermute | solution.py:25
  134.1 17.1 %collective-permute-start.3 = (bf16[114,2304]{1,0:T(8,128)(2,1)S(1)}, bf16[114,2304]{1,0:T(8,128)(2,1)}, u32[]{:S(2)}, u32[]{:S(2)}) collective-permute-start(bf16[114,2304]{1,0:T(8,128)(2,1)S(1)} %slice.92), channel_id=1, source_target_pairs={{0,4},{1,5},{2,6},{3,7},{4,8},{5,9},{6,10},{7,11},{8,12},{9,13},{1... | collective-permute-start | bytes 1575944 | tf_op jit(solution)/shard_map/ppermute | solution.py:25
  155.1 28.4 %collective-permute-start.1 = (bf16[114,2304]{1,0:T(8,128)(2,1)S(1)}, bf16[114,2304]{1,0:T(8,128)(2,1)}, u32[]{:S(2)}, u32[]{:S(2)}) collective-permute-start(bf16[114,2304]{1,0:T(8,128)(2,1)S(1)} %slice.92), channel_id=1, source_target_pairs={{0,6},{1,7},{2,8},{3,9},{4,10},{5,11},{6,12},{7,13},{8,14},{9,15},... | collective-permute-start | bytes 1575944 | tf_op jit(solution)/shard_map/ppermute | solution.py:25
  183.5 8.1 collective-permute-start
  194.2 19.4 %collective-permute-done.1 = bf16[114,2304]{1,0:T(8,128)(2,1)} collective-permute-done((bf16[114,2304]{1,0:T(8,128)(2,1)S(1)}, bf16[114,2304]{1,0:T(8,128)(2,1)}, u32[]{:S(2)}, u32[]{:S(2)}) %collective-permute-start.1) | collective-permute-done | bytes 525344 | tf_op jit(solution)/shard_map/ppermute | solution.py:25
  213.6 21.3 %collective-permute-done = bf16[114,2304]{1,0:T(8,128)(2,1)} collective-permute-done((bf16[114,2304]{1,0:T(8,128)(2,1)S(1)}, bf16[114,2304]{1,0:T(8,128)(2,1)}, u32[]{:S(2)}, u32[]{:S(2)}) %collective-permute-start) | collective-permute-done | bytes 525344 | tf_op jit(solution)/shard_map/ppermute | solution.py:25
  234.9 57.8 %concatenate.14 = bf16[1710,2304]{1,0:T(8,128)(2,1)} concatenate(bf16[114,2304]{1,0:T(8,128)(2,1)} %collective-permute-done, bf16[114,2304]{1,0:T(8,128)(2,1)} %collective-permute-done.1, bf16[114,2304]{1,0:T(8,128)(2,1)} %collective-permute-done.2, bf16[114,2304]{1,0:T(8,128)(2,1)} %collective-permute-done.3, bf16[114,2304]{1,0:T(8,128)(2,1)} %collective-permute-done.4, ...), dimensions={0} | concatenate | bytes 15759360 | tf_op jit(solution)/shard_map/concatenate | solution.py:140
  292.7 18.3 %gather_fusion = bf16[1458,2304]{1,0:T(8,128)(2,1)} fusion(bf16[1710,2304]{1,0:T(8,128)(2,1)} %concatenate.14, s32[2048]{0:T(1024)S(1)} %pad_clamp_fusion), kind=kCustom, calls=%fused_computation | custom fusion | bytes 13442760 | tf_op jit(solution)/shard_map/gather | solution.py:141
  344.5 11.7 reshape.334
  363.5 12.0 reshape.336
  395.6 11.5 fusion.70
  414.1 7.9 copy.60
  436.6 30.0 %scatter_custom_fusion = f32[1710,2304]{1,0:T(8,128)} fusion(s32[1458]{0:T(1024)} %copy-done.43, f32[1458,1152]{1,0:T(8,128)} %copy.60, f32[]{:T(128)} %constant.83.clone.1, f32[1458,1152]{1,0:T(8,128)} %copy.59, f32[]{:T(128)} %constant.37.clone.1), kind=kCustom, calls=%fused_computation.2 | custom fusion | flops 6718464 | bytes 29252608 | tf_op jit(solution)/shard_map/scatter-add | solution.py:199
  466.6 10.2 fusion.76
  497.1 13.1 %collective-permute-done.27 = f32[114,2304]{1,0:T(8,128)S(1)} collective-permute-done((f32[114,2304]{1,0:T(8,128)S(1)}, f32[114,2304]{1,0:T(8,128)S(1)}, u32[]{:S(2)}, u32[]{:S(2)}) %collective-permute-start.27) | collective-permute-done | bytes 1050656 | tf_op jit(solution)/shard_map/ppermute | solution.py:25
  512.5 21.4 %collective-permute-done.26 = f32[114,2304]{1,0:T(8,128)S(1)} collective-permute-done((f32[114,2304]{1,0:T(8,128)S(1)}, f32[114,2304]{1,0:T(8,128)S(1)}, u32[]{:S(2)}, u32[]{:S(2)}) %collective-permute-start.26) | collective-permute-done | bytes 1050656 | tf_op jit(solution)/shard_map/ppermute | solution.py:25
  536.2 16.0 %collective-permute-done.25 = f32[114,2304]{1,0:T(8,128)S(1)} collective-permute-done((f32[114,2304]{1,0:T(8,128)S(1)}, f32[114,2304]{1,0:T(8,128)S(1)}, u32[]{:S(2)}, u32[]{:S(2)}) %collective-permute-start.25) | collective-permute-done | bytes 1050656 | tf_op jit(solution)/shard_map/ppermute | solution.py:25
  555.4 20.5 %collective-permute-done.24 = f32[114,2304]{1,0:T(8,128)} collective-permute-done((f32[114,2304]{1,0:T(8,128)}, f32[114,2304]{1,0:T(8,128)}, u32[]{:S(2)}, u32[]{:S(2)}) %collective-permute-start.24) | collective-permute-done | bytes 1050656 | tf_op jit(solution)/shard_map/ppermute | solution.py:25
  578.6 32.5 %collective-permute-done.22 = f32[114,2304]{1,0:T(8,128)} collective-permute-done((f32[114,2304]{1,0:T(8,128)}, f32[114,2304]{1,0:T(8,128)}, u32[]{:S(2)}, u32[]{:S(2)}) %collective-permute-start.22) | collective-permute-done | bytes 1050656 | tf_op jit(solution)/shard_map/ppermute | solution.py:25
  622.6 10.4 collective-permute-done.19
  633.5 61.3 %collective-permute-done.17 = f32[114,2304]{1,0:T(8,128)} collective-permute-done((f32[114,2304]{1,0:T(8,128)}, f32[114,2304]{1,0:T(8,128)}, u32[]{:S(2)}, u32[]{:S(2)}) %collective-permute-start.17) | collective-permute-done | bytes 1050656 | tf_op jit(solution)/shard_map/ppermute | solution.py:25
  717.9 66.9 %all-to-all-start = ((bf16[4,114,1152]{2,1,0:T(8,128)(2,1)}), bf16[4,114,1152]{2,1,0:T(8,128)(2,1)S(1)}, u32[]{:S(2)}, u32[]{:S(2)}) async-start(bf16[4,114,1152]{2,1,0:T(8,128)(2,1)} %stack.10), calls=%async_computation | async-start | bytes 2211840 | tf_op jit(solution)/shard_map/all_to_all | solution.py:17
  784.8 27.5 %all-to-all-done = bf16[4,114,1152]{2,1,0:T(8,128)(2,1)S(1)} async-done(((bf16[4,114,1152]{2,1,0:T(8,128)(2,1)}), bf16[4,114,1152]{2,1,0:T(8,128)(2,1)S(1)}, u32[]{:S(2)}, u32[]{:S(2)}) %all-to-all-start) | async-done | bytes 1050656 | tf_op jit(solution)/shard_map/all_to_all | solution.py:17
  823.1 9.4 all-gather.37.cloned.1.call-done
  834.0 34.4 %all-gather.35.cloned.1.call-done = bf16[4,114,4304]{2,1,0:T(8,128)(2,1)} async-done(((bf16[1,114,4304]{2,1,0:T(8,128)(2,1)}), bf16[4,114,4304]{2,1,0:T(8,128)(2,1)}) %all-gather.35.cloned.1.call-update) | async-done | bytes 3925264 | tf_op jit(solution)/shard_map/all_gather | solution.py:58
  881.1 30.0 %all_to_all.10 = bf16[4,114,1152]{2,1,0:T(8,128)(2,1)S(1)} all-to-all(bf16[4,114,1152]{2,1,0:T(8,128)(2,1)S(1)} %stack.27), channel_id=1, replica_groups=mesh['rep'=8,'grp'=4] {'grp'}, dimensions={0} | all-to-all | bytes 2101248 | tf_op jit(solution)/shard_map/all_to_all | solution.py:17
  942.2 41.9 %all-reduce = (f32[1152]{0:T(1024)}, f32[1152]{0:T(1024)}, f32[2,1152]{1,0:T(2,128)}, f32[1152]{0:T(1024)}, f32[1152]{0:T(1024)}, /*index=5*/f32[1152]{0:T(1024)}, f32[4304]{0:T(1024)}, f32[1152]{0:T(1024)}) all-reduce(f32[1152]{0:T(1024)S(1)} %get-tuple-element.16, ...), channel_id=1, replica_groups=mesh['rep'=8,'grp'=4] {'rep','grp'}, use_global_device_ids=true, to_apply=%region_16.17 | all-reduce | flops 13520 | bytes 108160 | tf_op jit(solution)/shard_map/psum | solution.py:214
  986.6 90.9 %reduce-scatter.5.cloned.1.call-done = f32[864,144]{0,1:T(8,128)} async-done(((f32[864,1152]{0,1:T(8,128)}), f32[864,144]{0,1:T(8,128)}) %reduce-scatter.5.cloned.1.call-update) | async-done | bytes 497680 | tf_op jit(solution)/shard_map/reduce_scatter | solution.py:74
  1077.5 108.3 %reduce-scatter.11.cloned.1.call-done = f32[1076,144]{0,1:T(8,128)} async-done(((f32[1076,1152]{0,1:T(8,128)}), f32[1076,144]{0,1:T(8,128)}) %reduce-scatter.11.cloned.1.call-update) | async-done | bytes 619792 | tf_op jit(solution)/shard_map/reduce_scatter | solution.py:75
  1185.8 108.2 %reduce-scatter.9.cloned.1.call-done = f32[1076,144]{0,1:T(8,128)} async-done(((f32[1076,1152]{0,1:T(8,128)}), f32[1076,144]{0,1:T(8,128)}) %reduce-scatter.9.cloned.1.call-update) | async-done | bytes 619792 | tf_op jit(solution)/shard_map/reduce_scatter | solution.py:74
  (293 shorter events, 249.4 us)
Async XLA Ops:
  7.2 61.0 %all-gather.19.cloned.1.call-start = ((), (), s32[]{:S(2)}) async-start(), calls=%async_computation.6 | async-start | bytes 9953280 | tf_op jit(solution)/shard_map/all_gather | solution.py:122
  7.9 333.5 %all-gather.21.cloned.1.call-start = ((), (), s32[]{:S(2)}) async-start(), calls=%async_computation.7 | async-start | bytes 3317760 | tf_op jit(solution)/shard_map/all_gather | solution.py:123
  8.7 335.8 %all-gather.23.cloned.1.call-start = ((), (), s32[]{:S(2)}) async-start(), calls=%async_computation.12 | async-start | bytes 12441600 | tf_op jit(solution)/shard_map/all_gather | solution.py:124
  9.4 354.1 %all-gather.25.cloned.1.call-start = ((), (), s32[]{:S(2)}) async-start(), calls=%async_computation.13 | async-start | bytes 12441600 | tf_op jit(solution)/shard_map/all_gather | solution.py:125
  10.0 701.4 %all-gather.29.cloned.1.call-start = ((), (), s32[]{:S(2)}) async-start(), calls=%async_computation.15 | async-start | bytes 1382400 | tf_op jit(solution)/shard_map/all_gather | solution.py:58
  120.8 62.7 %collective-permute-start.5 = (bf16[114,2304]{1,0:T(8,128)(2,1)S(1)}, bf16[114,2304]{1,0:T(8,128)(2,1)S(1)}, u32[]{:S(2)}, u32[]{:S(2)}) collective-permute-start(bf16[114,2304]{1,0:T(8,128)(2,1)S(1)} %slice.92), channel_id=1, source_target_pairs={{0,2},{1,3},{2,4},{3,5},{4,6},{5,7},{6,8},{7,9},{8,10},{9,11},{10,... | collective-permute-start | bytes 1575944 | tf_op jit(solution)/shard_map/ppermute | solution.py:25
  128.2 66.0 %collective-permute-start.4 = (bf16[114,2304]{1,0:T(8,128)(2,1)S(1)}, bf16[114,2304]{1,0:T(8,128)(2,1)}, u32[]{:S(2)}, u32[]{:S(2)}) collective-permute-start(bf16[114,2304]{1,0:T(8,128)(2,1)S(1)} %slice.92), channel_id=1, source_target_pairs={{0,3},{1,4},{2,5},{3,6},{4,7},{5,8},{6,9},{7,10},{8,11},{9,12},{10... | collective-permute-start | bytes 1575944 | tf_op jit(solution)/shard_map/ppermute | solution.py:25
  134.1 60.1 %collective-permute-start.3 = (bf16[114,2304]{1,0:T(8,128)(2,1)S(1)}, bf16[114,2304]{1,0:T(8,128)(2,1)}, u32[]{:S(2)}, u32[]{:S(2)}) collective-permute-start(bf16[114,2304]{1,0:T(8,128)(2,1)S(1)} %slice.92), channel_id=1, source_target_pairs={{0,4},{1,5},{2,6},{3,7},{4,8},{5,9},{6,10},{7,11},{8,12},{9,13},{1... | collective-permute-start | bytes 1575944 | tf_op jit(solution)/shard_map/ppermute | solution.py:25
  155.1 58.5 %collective-permute-start.1 = (bf16[114,2304]{1,0:T(8,128)(2,1)S(1)}, bf16[114,2304]{1,0:T(8,128)(2,1)}, u32[]{:S(2)}, u32[]{:S(2)}) collective-permute-start(bf16[114,2304]{1,0:T(8,128)(2,1)S(1)} %slice.92), channel_id=1, source_target_pairs={{0,6},{1,7},{2,8},{3,9},{4,10},{5,11},{6,12},{7,13},{8,14},{9,15},... | collective-permute-start | bytes 1575944 | tf_op jit(solution)/shard_map/ppermute | solution.py:25
  183.5 51.4 %collective-permute-start = (bf16[114,2304]{1,0:T(8,128)(2,1)S(1)}, bf16[114,2304]{1,0:T(8,128)(2,1)}, u32[]{:S(2)}, u32[]{:S(2)}) collective-permute-start(bf16[114,2304]{1,0:T(8,128)(2,1)S(1)} %slice.92), channel_id=1, source_target_pairs={{0,7},{1,8},{2,9},{3,10},{4,11},{5,12},{6,13},{7,14},{8,15},{9,16}... | collective-permute-start | bytes 1575944 | tf_op jit(solution)/shard_map/ppermute | solution.py:25
  483.7 50.2 %collective-permute-start.26 = (f32[114,2304]{1,0:T(8,128)S(1)}, f32[114,2304]{1,0:T(8,128)S(1)}, u32[]{:S(2)}, u32[]{:S(2)}) collective-permute-start(f32[114,2304]{1,0:T(8,128)S(1)} %get-tuple-element.42), channel_id=1, source_target_pairs={{0,6},{1,7},{2,8},{3,9},{4,10},{5,11},{6,12},{7,13},{8,14},{9,15},... | collective-permute-start | bytes 3151880 | tf_op jit(solution)/shard_map/ppermute | solution.py:25
  485.1 67.1 %collective-permute-start.25 = (f32[114,2304]{1,0:T(8,128)S(1)}, f32[114,2304]{1,0:T(8,128)S(1)}, u32[]{:S(2)}, u32[]{:S(2)}) collective-permute-start(f32[114,2304]{1,0:T(8,128)S(1)} %get-tuple-element.43), channel_id=1, source_target_pairs={{0,5},{1,6},{2,7},{3,8},{4,9},{5,10},{6,11},{7,12},{8,13},{9,14},{... | collective-permute-start | bytes 3151880 | tf_op jit(solution)/shard_map/ppermute | solution.py:25
  486.5 89.5 %collective-permute-start.24 = (f32[114,2304]{1,0:T(8,128)}, f32[114,2304]{1,0:T(8,128)}, u32[]{:S(2)}, u32[]{:S(2)}) collective-permute-start(f32[114,2304]{1,0:T(8,128)} %get-tuple-element.44), channel_id=1, source_target_pairs={{0,4},{1,5},{2,6},{3,7},{4,8},{5,9},{6,10},{7,11},{8,12},{9,13},{1... | collective-permute-start | bytes 3151880 | tf_op jit(solution)/shard_map/ppermute | solution.py:25
  494.8 82.5 %collective-permute-start.23 = (f32[114,2304]{1,0:T(8,128)}, f32[114,2304]{1,0:T(8,128)}, u32[]{:S(2)}, u32[]{:S(2)}) collective-permute-start(f32[114,2304]{1,0:T(8,128)} %get-tuple-element.45), channel_id=1, source_target_pairs={{0,3},{1,4},{2,5},{3,6},{4,7},{5,8},{6,9},{7,10},{8,11},{9,12},{10... | collective-permute-start | bytes 3151880 | tf_op jit(solution)/shard_map/ppermute | solution.py:25
  510.2 100.8 %collective-permute-start.22 = (f32[114,2304]{1,0:T(8,128)}, f32[114,2304]{1,0:T(8,128)}, u32[]{:S(2)}, u32[]{:S(2)}) collective-permute-start(f32[114,2304]{1,0:T(8,128)} %get-tuple-element.46), channel_id=1, source_target_pairs={{0,2},{1,3},{2,4},{3,5},{4,6},{5,7},{6,8},{7,9},{8,10},{9,11},{10,... | collective-permute-start | bytes 3151880 | tf_op jit(solution)/shard_map/ppermute | solution.py:25
  533.9 78.4 %collective-permute-start.21 = (f32[114,2304]{1,0:T(8,128)}, f32[114,2304]{1,0:T(8,128)}, u32[]{:S(2)}, u32[]{:S(2)}) collective-permute-start(f32[114,2304]{1,0:T(8,128)} %get-tuple-element.47), channel_id=1, source_target_pairs={{0,1},{1,2},{2,3},{3,4},{4,5},{5,6},{6,7},{7,8},{8,9},{9,10},{10,1... | collective-permute-start | bytes 3151880 | tf_op jit(solution)/shard_map/ppermute | solution.py:25
  552.2 61.5 %collective-permute-start.20 = (f32[114,2304]{1,0:T(8,128)}, f32[114,2304]{1,0:T(8,128)}, u32[]{:S(2)}, u32[]{:S(2)}) collective-permute-start(f32[114,2304]{1,0:T(8,128)} %get-tuple-element.48), channel_id=1, source_target_pairs={{1,0},{2,1},{3,2},{4,3},{5,4},{6,5},{7,6},{8,7},{9,8},{10,9},{11,1... | collective-permute-start | bytes 3151880 | tf_op jit(solution)/shard_map/ppermute | solution.py:25
  555.4 157.5 %all-gather.31.cloned.1.call-start = ((), (), s32[]{:S(2)}) async-start(), calls=%async_computation.16 | async-start | bytes 1382400 | tf_op jit(solution)/shard_map/all_gather | solution.py:59
  576.0 57.0 %collective-permute-start.19 = (f32[114,2304]{1,0:T(8,128)}, f32[114,2304]{1,0:T(8,128)}, u32[]{:S(2)}, u32[]{:S(2)}) collective-permute-start(f32[114,2304]{1,0:T(8,128)} %get-tuple-element.49), channel_id=1, source_target_pairs={{2,0},{3,1},{4,2},{5,3},{6,4},{7,5},{8,6},{9,7},{10,8},{11,9},{12,... | collective-permute-start | bytes 3151880 | tf_op jit(solution)/shard_map/ppermute | solution.py:25
  577.3 56.2 %collective-permute-start.18 = (f32[114,2304]{1,0:T(8,128)}, f32[114,2304]{1,0:T(8,128)}, u32[]{:S(2)}, u32[]{:S(2)}) collective-permute-start(f32[114,2304]{1,0:T(8,128)} %get-tuple-element.50), channel_id=1, source_target_pairs={{3,0},{4,1},{5,2},{6,3},{7,4},{8,5},{9,6},{10,7},{11,8},{12,9},{13... | collective-permute-start | bytes 3151880 | tf_op jit(solution)/shard_map/ppermute | solution.py:25
  611.1 83.7 %collective-permute-start.17 = (f32[114,2304]{1,0:T(8,128)}, f32[114,2304]{1,0:T(8,128)}, u32[]{:S(2)}, u32[]{:S(2)}) collective-permute-start(f32[114,2304]{1,0:T(8,128)} %get-tuple-element.51), channel_id=1, source_target_pairs={{4,0},{5,1},{6,2},{7,3},{8,4},{9,5},{10,6},{11,7},{12,8},{13,9},{1... | collective-permute-start | bytes 3151880 | tf_op jit(solution)/shard_map/ppermute | solution.py:25
  612.4 83.8 %collective-permute-start.16 = (f32[114,2304]{1,0:T(8,128)}, f32[114,2304]{1,0:T(8,128)}, u32[]{:S(2)}, u32[]{:S(2)}) collective-permute-start(f32[114,2304]{1,0:T(8,128)} %get-tuple-element.52), channel_id=1, source_target_pairs={{5,0},{6,1},{7,2},{8,3},{9,4},{10,5},{11,6},{12,7},{13,8},{14,9},{... | collective-permute-start | bytes 3151880 | tf_op jit(solution)/shard_map/ppermute | solution.py:25
  613.7 82.5 %collective-permute-start.15 = (f32[114,2304]{1,0:T(8,128)}, f32[114,2304]{1,0:T(8,128)}, u32[]{:S(2)}, u32[]{:S(2)}) collective-permute-start(f32[114,2304]{1,0:T(8,128)} %get-tuple-element.53), channel_id=1, source_target_pairs={{6,0},{7,1},{8,2},{9,3},{10,4},{11,5},{12,6},{13,7},{14,8},{15,9},... | collective-permute-start | bytes 3151880 | tf_op jit(solution)/shard_map/ppermute | solution.py:25
  622.5 193.0 %all-gather.27.cloned.1.call-start = ((), (), s32[]{:S(2)}) async-start(), calls=%async_computation.14 | async-start | bytes 4147200 | tf_op jit(solution)/shard_map/all_gather | solution.py:56
  705.7 126.7 %all-gather.37.cloned.1.call-start = ((), (), s32[]{:S(2)}) async-start(), calls=%async_computation.19 | async-start | bytes 1382400 | tf_op jit(solution)/shard_map/all_gather | solution.py:59
  706.6 161.8 %all-gather.35.cloned.1.call-start = ((), (), s32[]{:S(2)}) async-start(), calls=%async_computation.18 | async-start | bytes 5222400 | tf_op jit(solution)/shard_map/all_gather | solution.py:58
  710.1 206.0 %all-gather.33.cloned.1.call-start = ((), (), s32[]{:S(2)}) async-start(), calls=%async_computation.17 | async-start | bytes 5222400 | tf_op jit(solution)/shard_map/all_gather | solution.py:56
  711.3 275.3 %reduce-scatter.7.cloned.1.call-start = ((), (), s32[]{:S(2)}) async-start(), calls=%async_computation.9 | async-start | bytes 1990656 | tf_op jit(solution)/shard_map/reduce_scatter | solution.py:75
  717.9 94.4 %all-to-all-start = ((bf16[4,114,1152]{2,1,0:T(8,128)(2,1)}), bf16[4,114,1152]{2,1,0:T(8,128)(2,1)S(1)}, u32[]{:S(2)}, u32[]{:S(2)}) async-start(bf16[4,114,1152]{2,1,0:T(8,128)(2,1)} %stack.10), calls=%async_computation | async-start | bytes 2211840 | tf_op jit(solution)/shard_map/all_to_all | solution.py:17
  784.8 292.7 %reduce-scatter.5.cloned.1.call-start = ((), (), s32[]{:S(2)}) async-start(), calls=%async_computation.8 | async-start | bytes 4644864 | tf_op jit(solution)/shard_map/reduce_scatter | solution.py:74
  823.0 362.8 %reduce-scatter.11.cloned.1.call-start = ((), (), s32[]{:S(2)}) async-start(), calls=%async_computation.11 | async-start | bytes 5971968 | tf_op jit(solution)/shard_map/reduce_scatter | solution.py:75
  880.1 413.9 %reduce-scatter.9.cloned.1.call-start = ((), (), s32[]{:S(2)}) async-start(), calls=%async_computation.10 | async-start | bytes 5971968 | tf_op jit(solution)/shard_map/reduce_scatter | solution.py:74
  (73 other events, 1578.7 us)
Sparse Core Ops, SparseCore 0:
  9.5 58.5 all-gather.18
  69.7 59.2 all-gather.20
  130.6 116.7 all-gather.22
  248.8 68.6 all-gather.24
  555.5 44.1 all-gather.28
  622.6 47.9 all-gather.30
  705.8 109.6 all-gather.26
  817.7 14.7 all-gather.36
  834.0 34.3 all-gather.34
  869.8 46.2 all-gather.32
  920.1 66.4 reduce-scatter.6
  990.6 86.8 reduce-scatter.4
  1081.7 104.1 reduce-scatter.10
  1189.8 104.1 reduce-scatter.8
